TPU v7x, 512 devices: a whole 4x8x8 slice. The times are simulated.
512 devices in a mesh: dp: 4 (over x), ep: 128 (over z, y, core).
Axes of the slice: x: 4, y: 8, z: 8, core: 2. Of those that a mesh axis runs over, the one named last changes fastest.
Arguments:
- tokens: bfloat16 [128, 16, 2048], P('ep', 'dp'), may hold values from -6 to 6
- dest_ids: int32 [128, 16, 8], P('ep', 'dp'), may hold values from 0 to 127, all different within a row; in each aligned block of 16 rows (0 to 15, 16 to 31, ..., all dimensions but the last counted through in order) at most 2 rows name the same one
- gate_fixed: int32 [128, 16, 8], P('ep', 'dp'), may hold values from 1 to 65535
- gate_up: bfloat16 [128, 2, 768, 2048], P('ep', None, 'dp'), may hold values from -0.125 to 0.125
- down: bfloat16 [128, 768, 2048], P('ep', 'dp'), may hold values from -0.21875 to 0.21875
Outputs:
- mixed: bfloat16 [128, 16, 2048], P('ep', 'dp')
Inputs may be any that keep to these rules, and one draw needn't show every extreme that they name: `dest_ids`: each row names 8 different experts; within one column's 16 rows no expert is named by more than 2 routes.
All inputs are finite; a program needn't handle non-finite values.
Results may differ from a plain program's by a relative error of at most 0.012.
Values may be sent and summed in bfloat16 or wider, within the bound.
A program may use at most 192 MiB of HBM per device.

v0:
```python
import jax
import jax.numpy as jnp
from jax import lax
from jax.sharding import PartitionSpec as P


def feed_forward(rows, pair, lower):
    gate = jnp.einsum("nd,hd->nh", rows, pair[0], preferred_element_type=jnp.float32)
    upper = jnp.einsum("nd,hd->nh", rows, pair[1], preferred_element_type=jnp.float32)
    hidden = (jax.nn.silu(gate) * upper).astype(jnp.bfloat16)
    return jnp.dot(hidden, lower, preferred_element_type=jnp.float32).astype(jnp.bfloat16)


def per_device(tokens, dest_ids, gate_fixed, gate_up, down):
    peer_count = lax.axis_size("ep")
    own_rows = tokens[0]
    width = own_rows.shape[1]
    top_count = dest_ids.shape[2]
    route_table = jnp.concatenate([dest_ids[0], gate_fixed[0]], axis=1)
    column_table = lax.all_gather(route_table, "dp", axis=0, tiled=True)
    col_rows = column_table.shape[0]
    capacity = min(col_rows, max(2, 2 * col_rows * top_count // peer_count))
    target_dev = column_table[:, :top_count].reshape(-1)
    gate_raw = column_table[:, top_count:].astype(jnp.float32)
    gate_norm = gate_raw / jnp.sum(gate_raw, axis=1, keepdims=True)
    marks = (target_dev[:, None] == jnp.arange(peer_count, dtype=jnp.int32)[None, :]).astype(
        jnp.int32
    )
    slot_rank = jnp.sum(jnp.cumsum(marks, axis=0) * marks, axis=1) - 1
    slot_index = target_dev * capacity + slot_rank
    source_row = jnp.arange(target_dev.shape[0], dtype=jnp.int32) // top_count
    column_rows = lax.all_gather(own_rows, "dp", axis=0, tiled=True)
    send_block = (
        jnp.zeros((peer_count * capacity, width), jnp.bfloat16)
        .at[slot_index]
        .set(column_rows[source_row])
        .reshape(peer_count, capacity, width)
    )
    rows = lax.all_to_all(send_block, "ep", split_axis=0, concat_axis=0, tiled=True)
    flat_rows = rows.reshape(-1, rows.shape[2])
    own_out = feed_forward(flat_rows, gate_up[0], down[0])
    returned = lax.all_to_all(
        own_out.reshape(rows.shape[0], rows.shape[1], -1),
        "ep",
        split_axis=0,
        concat_axis=0,
        tiled=True,
    )
    flat_back = returned.reshape(peer_count * capacity, -1)
    weighted = flat_back[slot_index].astype(jnp.float32) * gate_norm.reshape(-1)[:, None]
    summed = jnp.sum(weighted.reshape(col_rows, top_count, -1), axis=1)
    mine = lax.psum_scatter(summed.astype(jnp.bfloat16), "dp", scatter_dimension=0, tiled=True)
    return mine[None]


def solution(mesh):
    return jax.shard_map(
        per_device,
        mesh=mesh,
        in_specs=(
            P("ep", "dp", None),
            P("ep", "dp", None),
            P("ep", "dp", None),
            P("ep", None, "dp", None),
            P("ep", "dp", None),
        ),
        out_specs=P("ep", "dp", None),
        check_vma=False,
    )
```

profile of v0, /device:TPU:1, one launch (start us, length us, event | category | flops | bytes accessed | tf_op | source)
XLA Modules:
  0.0 181.7 jit_solution(7191116500669155721)
XLA Ops:
  6.5 0.0 copy-start
  6.5 0.8 add_bitcast_fusion
  7.4 9.3 %all-gather.1 = s32[4,4,16]{2,1,0:T(4,128)S(1)} all-gather(s32[1,4,16]{2,1,0:T(4,128)S(1)} %add_bitcast_fusion), channel_id=1, replica_groups=mesh['dp'=4,'ep'=128] {'dp'}, dimensions={0}, use_global_device_ids=true | all-gather | bytes 1280 | tf_op jit(solution)/shard_map/all_gather | solution.py:20
  16.7 0.1 eq.15
  16.8 0.1 fusion.19
  16.9 0.2 reduce_window_sum.11
  17.1 0.2 select_reduce_fusion
  17.2 0.1 mul.37
  17.3 0.7 copy.7
  18.1 9.1 %all-gather = bf16[1,16,2048]{2,0,1:T(2,128)(2,1)S(1)} all-gather(bf16[1,4,2048]{2,0,1:T(2,128)(2,1)S(1)} %copy.7), channel_id=2, replica_groups=mesh['dp'=4,'ep'=128] {'dp'}, dimensions={1}, use_global_device_ids=true | all-gather | bytes 81920 | tf_op jit(solution)/shard_map/all_gather | solution.py:32
  27.3 3.4 %scatter_custom_fusion = bf16[256,2048]{1,0:T(8,128)(2,1)S(1)} fusion(s32[128]{0:T(128)S(1)} %fusion.23, bf16[16,2048]{1,0:T(8,128)(2,1)S(1)} %bitcast.37, s32[1024]{0:T(1024)S(1)} %pad_clamp_fusion.1, bf16[]{:T(256)} %constant.28.clone.1), kind=kCustom, calls=%fused_computation.14 | custom fusion | bytes 1048578 | tf_op jit(solution)/shard_map/scatter | solution.py:36
  30.6 0.7 reshape.105
  31.3 53.9 %all_to_all.10 = bf16[128,2,2048]{2,1,0:T(2,128)(2,1)S(1)} all-to-all(bf16[128,2,2048]{2,1,0:T(2,128)(2,1)S(1)} %reshape.105), channel_id=1, replica_groups=mesh['dp'=4,'ep'=128] {'ep'}, dimensions={0} | all-to-all | bytes 2097152 | tf_op jit(solution)/shard_map/all_to_all | solution.py:39
  85.3 0.4 reshape.106
  85.7 1.6 fusion.5
  87.3 0.0 copy-done
  87.3 2.6 %convolution_convert_fusion = bf16[256,2048]{1,0:T(8,128)(2,1)S(1)} fusion(bf16[256,2048]{1,0:T(8,128)(2,1)S(1)} %reshape.106, bf16[1,192,2048]{2,1,0:T(8,128)(2,1)S(1)} %copy-done, bf16[1,2,192,2048]{3,2,1,0:T(8,128)(2,1)} %param.8, f32[256,192]{0,1:T(8,128)S(1)} %fusion.5), kind=kOutput, calls=%fused_computation.3 | convolution fusion | flops 403472384 | bytes 3866624 | tf_op jit(solution)/shard_map/dot_general | solution.py:11
  89.9 1.5 reshape.107
  91.4 6.4 %all-to-all-start.1 = ((bf16[128,2,2048]{2,1,0:T(2,128)(2,1)}), bf16[128,2,2048]{2,1,0:T(2,128)(2,1)S(1)}, u32[]{:S(2)}, u32[]{:S(2)}) async-start(bf16[128,2,2048]{2,1,0:T(2,128)(2,1)} %reshape.107), calls=%async_computation.1 | async-start | bytes 2097152 | tf_op jit(solution)/shard_map/all_to_all | solution.py:42
  97.8 0.0 all-reduce.3.cloned.1.call-start
  97.9 0.2 fusion.21
  98.1 0.1 fusion.20
  98.2 30.6 %all-to-all-done.1 = bf16[128,2,2048]{2,1,0:T(2,128)(2,1)S(1)} async-done(((bf16[128,2,2048]{2,1,0:T(2,128)(2,1)}), bf16[128,2,2048]{2,1,0:T(2,128)(2,1)S(1)}, u32[]{:S(2)}, u32[]{:S(2)}) %all-to-all-start.1) | async-done | bytes 1048608 | tf_op jit(solution)/shard_map/all_to_all | solution.py:42
  128.8 0.4 reshape.108
  129.2 0.9 gather_fusion
  130.2 1.1 fusion.1
  131.2 0.0 all-reduce.3.cloned.1.call-update
  131.3 1.3 dynamic-slice
  133.2 40.3 %all-reduce.3.cloned.1.call-done = bf16[16,2048]{1,0:T(8,128)(2,1)} async-done(((bf16[16,2048]{1,0:T(8,128)(2,1)}), bf16[16,2048]{1,0:T(8,128)(2,1)}) %all-reduce.3.cloned.1.call-update) | async-done | bytes 65552
  173.5 1.4 dynamic-slice_bitcast_fusion
  (6 shorter events, 0.1 us)
Async XLA Ops:
  6.5 80.8 %copy-start = (bf16[1,192,2048]{2,1,0:T(8,128)(2,1)S(1)}, bf16[1,192,2048]{2,1,0:T(8,128)(2,1)}, u32[]{:S(2)}) copy-start(bf16[1,192,2048]{2,1,0:T(8,128)(2,1)} %param.9) | copy-start | bytes 2359300
  91.4 37.4 %all-to-all-start.1 = ((bf16[128,2,2048]{2,1,0:T(2,128)(2,1)}), bf16[128,2,2048]{2,1,0:T(2,128)(2,1)S(1)}, u32[]{:S(2)}, u32[]{:S(2)}) async-start(bf16[128,2,2048]{2,1,0:T(2,128)(2,1)} %reshape.107), calls=%async_computation.1 | async-start | bytes 2097152 | tf_op jit(solution)/shard_map/all_to_all | solution.py:42
  97.8 75.7 %all-reduce.3.cloned.1.call-start = ((), (), s32[]{:S(2)}) async-start(), calls=%async_computation.2 | async-start | bytes 131072
Sparse Core Ops, SparseCore 0:
  131.4 42.0 all-reduce.2
where the time goes:
time: 183 us; the launch traced here: 182 us
  blocking collectives  72.3 us (40%)
  waiting for transfers between devices  71 us (39%)
  between operations  14.2 us (8%)
  local copies, waits for them, and re-layouts  11 us (6%)
  starting transfers between devices  6.45 us (4%)
  matrix products  4.21 us (2%)
  other arithmetic  2.64 us (1%)
    all_to_all x1, blocking collectives, per_device(): lax.all_to_all(send_block, 'ep', split_axis=0, concat_axis=0, tiled=True)  53.9 us
    unnamed x2, waiting for transfers between devices  40.3 us
    all_to_all x1, waiting for transfers between devices, per_device(): lax.all_to_all(own_out.reshape(rows.shape[0], rows.shape[1], -1), 'ep', s...  30.6 us
    all_gather x1, blocking collectives, per_device(): column_table = lax.all_gather(route_table, 'dp', axis=0, tiled=True)  9.3 us
    all_gather x1, blocking collectives, per_device(): column_rows = lax.all_gather(own_rows, 'dp', axis=0, tiled=True)  9.11 us
    all_to_all x1, starting transfers between devices, per_device(): lax.all_to_all(own_out.reshape(rows.shape[0], rows.shape[1], -1), 'ep', s...  6.41 us
  transfers between devices with their start and end apart: 2, of which 2 were waited for; matrix products, arithmetic and copies ran while one was open for 1% of the time, Pallas kernels for 0%

commit v1 on v0

--- a/solution.py
+++ b/solution.py
@@ -16,8 +16,16 @@
     own_rows = tokens[0]
     width = own_rows.shape[1]
     top_count = dest_ids.shape[2]
-    route_table = jnp.concatenate([dest_ids[0], gate_fixed[0]], axis=1)
-    column_table = lax.all_gather(route_table, "dp", axis=0, tiled=True)
+    gates = gate_fixed[0]
+    route_table = jnp.concatenate([dest_ids[0], gates >> 8, gates & 255], axis=1)
+    route_pad = jnp.pad(route_table, ((0, 0), (0, 128 - 3 * top_count))).astype(jnp.bfloat16)
+    packed = lax.all_gather(jnp.concatenate([own_rows, route_pad], axis=1), "dp", axis=0, tiled=True)
+    column_rows = packed[:, :width]
+    table = packed[:, width : width + 3 * top_count].astype(jnp.int32)
+    column_table = jnp.concatenate(
+        [table[:, :top_count], table[:, top_count : 2 * top_count] * 256 + table[:, 2 * top_count :]],
+        axis=1,
+    )
     col_rows = column_table.shape[0]
     capacity = min(col_rows, max(2, 2 * col_rows * top_count // peer_count))
     target_dev = column_table[:, :top_count].reshape(-1)
@@ -29,7 +37,6 @@
     slot_rank = jnp.sum(jnp.cumsum(marks, axis=0) * marks, axis=1) - 1
     slot_index = target_dev * capacity + slot_rank
     source_row = jnp.arange(target_dev.shape[0], dtype=jnp.int32) // top_count
-    column_rows = lax.all_gather(own_rows, "dp", axis=0, tiled=True)
     send_block = (
         jnp.zeros((peer_count * capacity, width), jnp.bfloat16)
         .at[slot_index]
@@ -49,7 +56,10 @@
     flat_back = returned.reshape(peer_count * capacity, -1)
     weighted = flat_back[slot_index].astype(jnp.float32) * gate_norm.reshape(-1)[:, None]
     summed = jnp.sum(weighted.reshape(col_rows, top_count, -1), axis=1)
-    mine = lax.psum_scatter(summed.astype(jnp.bfloat16), "dp", scatter_dimension=0, tiled=True)
+    parts = lax.all_to_all(
+        summed.astype(jnp.bfloat16).reshape(4, -1, width), "dp", split_axis=0, concat_axis=0, tiled=True
+    )
+    mine = jnp.sum(parts.astype(jnp.float32), axis=0).astype(jnp.bfloat16)
     return mine[None]
 
 

time: 183 us -> 123 us (0.67)
  waiting for transfers between devices: 71 us -> 30.7 us
  between operations: 14.2 us -> 0.15 us
  local copies, waits for them, and re-layouts: 11 us -> 7.6 us
  blocking collectives: 72.3 us -> 69.1 us
    unnamed x2 -> x0, waiting for transfers between devices: 40.3 us -> none
    all_gather x2 -> x1, blocking collectives: 18.4 us -> 10.2 us  [per_device(): lax.all_gather(jnp.concatenate([own_rows, route_pad], axis=1), 'dp', axis...]
    all_to_all x0 -> x1, blocking collectives: none -> 7.66 us  [per_device(): lax.all_to_all(summed.astype(jnp.bfloat16).reshape(4, -1, width), 'dp', s...]
    all_to_all x1, blocking collectives: 53.9 us -> 51.2 us  [per_device(): lax.all_to_all(send_block, 'ep', split_axis=0, concat_axis=0, tiled=True)]
    unnamed x5 -> x3, local copies, waits for them, and re-layouts: 2.06 us -> 0.02 us
  transfers between devices with their start and end apart: 2 -> 1, of which waited for: 2 -> 1; matrix products, arithmetic and copies ran while one was open for 1% -> 0% of each run, Pallas kernels for 0% -> 0%
where the time goes in v1:
time: 123 us; the launch traced here: 122 us
  blocking collectives  69.1 us (56%)
  waiting for transfers between devices  30.7 us (25%)
  local copies, waits for them, and re-layouts  7.6 us (6%)
  starting transfers between devices  6.41 us (5%)
  matrix products  4.2 us (3%)
  other arithmetic  3.41 us (3%)
    all_to_all x1, blocking collectives, per_device(): lax.all_to_all(send_block, 'ep', split_axis=0, concat_axis=0, tiled=True)  51.2 us
    all_to_all x1, waiting for transfers between devices, per_device(): lax.all_to_all(own_out.reshape(rows.shape[0], rows.shape[1], -1), 'ep', s...  30.7 us
    all_gather x1, blocking collectives, per_device(): lax.all_gather(jnp.concatenate([own_rows, route_pad], axis=1), 'dp', axis...  10.2 us
    all_to_all x1, blocking collectives, per_device(): lax.all_to_all(summed.astype(jnp.bfloat16).reshape(4, -1, width), 'dp', s...  7.66 us
    all_to_all x1, starting transfers between devices, per_device(): lax.all_to_all(own_out.reshape(rows.shape[0], rows.shape[1], -1), 'ep', s...  6.41 us
    scatter x1, local copies, waits for them, and re-layouts, per_device(): send_block = jnp.zeros((peer_count * capacity, width), jnp.bfloat16).at[s...  3.36 us
    dot_general x1, matrix products, feed_forward(): jnp.dot(hidden, lower, preferred_element_type=jnp.float32)  2.57 us
  transfers between devices with their start and end apart: 1, of which 1 were waited for; matrix products, arithmetic and copies ran while one was open for 0% of the time, Pallas kernels for 0%

profile of v1, /device:TPU:1, one launch (start us, length us, event | category | flops | bytes accessed | tf_op | source)
XLA Modules:
  0.0 121.5 jit_solution(11102416586996701243)
XLA Ops:
  0.0 0.0 copy-start
  0.0 0.8 fusion.25
  0.8 0.1 fusion.28
  0.9 0.7 maximum_bitcast_fusion
  1.6 10.2 %all-gather = bf16[4,4,2176]{2,1,0:T(4,128)(2,1)S(1)} all-gather(bf16[1,4,2176]{2,1,0:T(4,128)(2,1)S(1)} %maximum_bitcast_fusion), channel_id=1, replica_groups=mesh['dp'=4,'ep'=128] {'dp'}, dimensions={0}, use_global_device_ids=true | all-gather | bytes 87040 | tf_op jit(solution)/shard_map/all_gather | solution.py:22
  11.8 0.1 eq.15
  11.9 0.1 fusion.19
  12.0 0.2 reduce_window_sum.11
  12.2 0.2 select_reduce_fusion
  12.4 0.1 mul.43
  12.5 3.4 %scatter_custom_fusion = bf16[256,2048]{1,0:T(8,128)(2,1)S(1)} fusion(s32[128]{0:T(128)S(1)} %fusion.30, bf16[16,2048]{1,0:T(8,128)(2,1)S(1)} %slice.36, s32[1024]{0:T(1024)S(1)} %pad_clamp_fusion.1, bf16[]{:T(256)} %constant.33.clone.1), kind=kCustom, calls=%fused_computation.14 | custom fusion | bytes 1048578 | tf_op jit(solution)/shard_map/scatter | solution.py:43
  15.8 0.7 reshape.114
  16.6 51.2 %all_to_all.15 = bf16[128,2,2048]{2,1,0:T(2,128)(2,1)S(1)} all-to-all(bf16[128,2,2048]{2,1,0:T(2,128)(2,1)S(1)} %reshape.114), channel_id=1, replica_groups=mesh['dp'=4,'ep'=128] {'ep'}, dimensions={0} | all-to-all | bytes 2097152 | tf_op jit(solution)/shard_map/all_to_all | solution.py:46
  67.8 0.4 reshape.115
  68.2 1.6 %fusion.5 = f32[256,192]{0,1:T(8,128)S(1)} fusion(bf16[256,2048]{1,0:T(8,128)(2,1)S(1)} %reshape.115, bf16[1,2,192,2048]{3,2,1,0:T(8,128)(2,1)} %param.8), kind=kOutput, calls=%fused_computation.10 | convolution fusion | flops 201326592 | bytes 2031616 | tf_op jit(solution)/shard_map/nd,hd->nh/dot_general | solution.py:8
  69.9 0.0 copy-done
  69.9 2.6 %convolution_convert_fusion = bf16[256,2048]{1,0:T(8,128)(2,1)S(1)} fusion(bf16[256,2048]{1,0:T(8,128)(2,1)S(1)} %reshape.115, bf16[1,192,2048]{2,1,0:T(8,128)(2,1)S(1)} %copy-done, bf16[1,2,192,2048]{3,2,1,0:T(8,128)(2,1)} %param.8, f32[256,192]{0,1:T(8,128)S(1)} %fusion.5), kind=kOutput, calls=%fused_computation.3 | convolution fusion | flops 403472384 | bytes 3866624 | tf_op jit(solution)/shard_map/dot_general | solution.py:11
  72.5 1.5 %reshape.116 = bf16[128,2,2048]{2,1,0:T(2,128)(2,1)} reshape(bf16[256,2048]{1,0:T(8,128)(2,1)S(1)} %convolution_convert_fusion) | data formatting | bytes 2097152 | tf_op jit(solution)/shard_map/reshape | solution.py:50
  74.0 6.4 %all-to-all-start.1 = ((bf16[128,2,2048]{2,1,0:T(2,128)(2,1)}), bf16[128,2,2048]{2,1,0:T(2,128)(2,1)S(1)}, u32[]{:S(2)}, u32[]{:S(2)}) async-start(bf16[128,2,2048]{2,1,0:T(2,128)(2,1)} %reshape.116), calls=%async_computation.1 | async-start | bytes 2097152 | tf_op jit(solution)/shard_map/all_to_all | solution.py:49
  80.4 0.2 fusion.21
  80.6 0.1 broadcast_divide_fusion
  80.7 30.7 %all-to-all-done.1 = bf16[128,2,2048]{2,1,0:T(2,128)(2,1)S(1)} async-done(((bf16[128,2,2048]{2,1,0:T(2,128)(2,1)}), bf16[128,2,2048]{2,1,0:T(2,128)(2,1)S(1)}, u32[]{:S(2)}, u32[]{:S(2)}) %all-to-all-start.1) | async-done | bytes 1048608 | tf_op jit(solution)/shard_map/all_to_all | solution.py:49
  111.4 0.4 reshape.117
  111.8 0.9 gather_fusion
  112.7 0.5 fusion.1
  113.2 7.7 %all_to_all.16 = bf16[4,4,2048]{2,1,0:T(4,128)(2,1)S(1)} all-to-all(bf16[4,4,2048]{2,1,0:T(4,128)(2,1)S(1)} %convert_element_type.40), channel_id=1, replica_groups=mesh['dp'=4,'ep'=128] {'dp'}, dimensions={0} | all-to-all | bytes 131072 | tf_op jit(solution)/shard_map/all_to_all | solution.py:59
  120.9 0.6 reduce_sum.42
  (9 shorter events, 0.1 us)
Async XLA Ops:
  0.0 69.9 %copy-start = (bf16[1,192,2048]{2,1,0:T(8,128)(2,1)S(1)}, bf16[1,192,2048]{2,1,0:T(8,128)(2,1)}, u32[]{:S(2)}) copy-start(bf16[1,192,2048]{2,1,0:T(8,128)(2,1)} %param.9) | copy-start | bytes 2359300
  74.0 37.4 %all-to-all-start.1 = ((bf16[128,2,2048]{2,1,0:T(2,128)(2,1)}), bf16[128,2,2048]{2,1,0:T(2,128)(2,1)S(1)}, u32[]{:S(2)}, u32[]{:S(2)}) async-start(bf16[128,2,2048]{2,1,0:T(2,128)(2,1)} %reshape.116), calls=%async_computation.1 | async-start | bytes 2097152 | tf_op jit(solution)/shard_map/all_to_all | solution.py:49

commit v2 on v0

v2 whole, which is shorter than its diff:
```python
import jax
import jax.numpy as jnp
from jax import lax
from jax.experimental import pallas as pl
from jax.experimental.pallas import tpu as pltpu
from jax.sharding import PartitionSpec as P

BF = jnp.bfloat16
F32 = jnp.float32
MESH = pl.DeviceIdType.MESH
PEERS = 128
DP = 4
TOP = 8
LANES = 128
QUARTER = 512
BLOCKS = PEERS // 16


def iota(shape, dim):
    return lax.broadcasted_iota(jnp.int32, shape, dim)


def permutation(inverse):
    moved = iota((128, 128), 1 if inverse else 0)
    place = iota((128, 128), 0 if inverse else 1)
    home = (moved & 31) // 2 * 8 + (moved & 1) * 4 + moved // 32
    return jnp.where(home == place, 1.0, 0.0).astype(BF)


def remote(src, dst, send_sem, recv_sem, device):
    return pltpu.make_async_remote_copy(
        src_ref=src, dst_ref=dst, send_sem=send_sem, recv_sem=recv_sem,
        device_id=device, device_id_type=MESH,
    )


def kernel(
    msg_ref, pair_hbm, lower_hbm, out_ref,
    got, pair, lower, send1, recv1, rows, part, pin, send2, back, outp, fin,
    local_sem, xs, xr, a_send, a_recv, gs, gr, rs, rr, b_send, b_recv, fs, fr, own_sem,
):
    q = lax.axis_index("dp")
    me = lax.axis_index("ep")
    load_pair = pltpu.make_async_copy(pair_hbm, pair, local_sem.at[0])
    load_lower = pltpu.make_async_copy(lower_hbm, lower, local_sem.at[1])
    load_pair.start()
    load_lower.start()

    barrier = pltpu.get_barrier_semaphore()
    for d in range(1, DP):
        pl.semaphore_signal(
            barrier, inc=1, device_id={"dp": lax.rem(q + d, DP)}, device_id_type=MESH
        )

    def greet(d, carry):
        pl.semaphore_signal(
            barrier, inc=1, device_id={"ep": lax.rem(me + d, PEERS)}, device_id_type=MESH
        )
        return carry

    lax.fori_loop(1, PEERS, greet, 0)
    pl.semaphore_wait(barrier, DP - 1 + PEERS - 1)

    copies = []
    for d in range(1, DP):
        to = lax.rem(q + d, DP)
        copies.append(
            remote(msg_ref.at[to], got.at[q], xs.at[d - 1], xr.at[d - 1], {"dp": to})
        )
        copies[-1].start()
    got[q] = msg_ref[q]
    for copy in copies:
        copy.wait()

    tok = jnp.concatenate([got[i, 0:16, :] for i in range(DP)], axis=0)
    table = jnp.concatenate([got[i, 16:32, :].astype(F32) for i in range(DP)], axis=0)
    wide = (64, PEERS * 8)
    column = iota(wide, 1)
    expert = (column // 8).astype(F32)
    named = jnp.zeros(wide, F32)
    high = jnp.zeros(wide, F32)
    low = jnp.zeros(wide, F32)
    total = jnp.zeros((64, 1), F32)
    for k in range(TOP):
        same = table[:, k : k + 1] == expert
        hi, lo = table[:, TOP + k : TOP + k + 1], table[:, 2 * TOP + k : 2 * TOP + k + 1]
        total = total + (hi * 256.0 + lo)
        named = jnp.where(same, 1.0, named)
        high = jnp.where(same, hi, high)
        low = jnp.where(same, lo, low)
    earlier = jnp.where(
        (iota((64, 64), 1) // 4 < iota((64, 64), 0) // 4) & ((iota((64, 64), 1) & 3) == 0), 1.0, 0.0
    ).astype(BF)
    rank = jnp.dot(earlier, named.astype(BF), preferred_element_type=F32)
    slot = ((column // 4) & 1).astype(F32)
    live = (rank == slot) & ((iota(wide, 0) & 3) == (column & 3))
    pick = jnp.where(live, named, 0.0)
    high = jnp.where(live, high, 0.0).astype(BF)
    low = jnp.where(live, low, 0.0).astype(BF)
    packed = jnp.dot(pick.T.astype(BF), tok, preferred_element_type=F32)
    send1[...] = packed.reshape(PEERS, 8, LANES).astype(BF)

    def dispatch(d, carry):
        to = lax.rem(me + d, PEERS)
        remote(send1.at[to], recv1.at[q, me], a_send, a_recv, {"ep": to}).start()
        return carry

    lax.fori_loop(1, PEERS, dispatch, 0)
    own = pltpu.make_async_copy(send1.at[me], recv1.at[q, me], own_sem.at[0])
    own.start()
    own.wait()
    whole = pl.ds(0, PEERS - 1)
    arrived = remote(
        send1.at[whole], recv1.at[q, whole], a_send, a_recv, {"ep": lax.rem(me + 1, PEERS)}
    )
    arrived.wait()

    copies = {}
    for d in (2, 1, 3):
        to = lax.rem(q + d, DP)
        copies[d] = remote(recv1.at[q], recv1.at[q], gs.at[d - 1], gr.at[d - 1], {"dp": to})
        copies[d].start()
    load_pair.wait()
    order = permutation(False)
    gate = jnp.zeros((PEERS * 2, pair.shape[1]), F32)
    upper = jnp.zeros((PEERS * 2, pair.shape[1]), F32)
    contract = (((1,), (1,)), ((), ()))
    for d in (0, 1, 3, 2):
        if d:
            copies[d].wait()
        src = lax.rem(q + DP - d, DP)
        for b in range(BLOCKS):
            block = recv1[src, b * 16 : (b + 1) * 16].astype(F32).reshape(128, LANES).astype(BF)
            moved = jnp.dot(order, block, preferred_element_type=F32).astype(BF)
            for j in range(4):
                rows[b * 32 : (b + 1) * 32, j * LANES : (j + 1) * LANES] = moved[j * 32 : (j + 1) * 32]
        x = rows[...]
        features = pl.ds(pl.multiple_of(src * QUARTER, QUARTER), QUARTER)
        gate = gate + lax.dot_general(x, pair[0, :, features], contract, preferred_element_type=F32)
        upper = upper + lax.dot_general(x, pair[1, :, features], contract, preferred_element_type=F32)
    hidden = (gate / (1.0 + jnp.exp(-gate)) * upper).astype(BF)
    load_lower.wait()

    copies = {}
    for d in (2, 1, 3, 0):
        to = lax.rem(q + d, DP)
        features = pl.ds(pl.multiple_of(to * QUARTER, QUARTER), QUARTER)
        part[to] = jnp.dot(hidden, lower[:, features], preferred_element_type=F32).astype(BF)
        if d:
            copies[d] = remote(part.at[to], pin.at[q], rs.at[d - 1], rr.at[d - 1], {"dp": to})
            copies[d].start()
    for d in (1, 3, 2):
        copies[d].wait()
    back_order = permutation(True)
    for b in range(BLOCKS):
        lines = slice(b * 32, (b + 1) * 32)
        added = part[q, lines].astype(F32)
        for d in range(1, DP):
            added = added + pin[lax.rem(q + DP - d, DP), lines].astype(F32)
        added = added.astype(BF)
        stacked = jnp.concatenate([added[:, j * LANES : (j + 1) * LANES] for j in range(4)], axis=0)
        moved = jnp.dot(back_order, stacked, preferred_element_type=F32)
        send2[b * 16 : (b + 1) * 16] = moved.reshape(16, 8, LANES).astype(BF)

    def giveback(d, carry):
        to = lax.rem(me + d, PEERS)
        remote(send2.at[to], back.at[me], b_send, b_recv, {"ep": to}).start()
        return carry

    lax.fori_loop(1, PEERS, giveback, 0)
    own = pltpu.make_async_copy(send2.at[me], back.at[me], own_sem.at[1])
    own.start()
    own.wait()
    arrived = remote(
        send2.at[whole], back.at[whole], b_send, b_recv, {"ep": lax.rem(me + 1, PEERS)}
    )
    arrived.wait()

    results = back[...].astype(F32).reshape(PEERS * 8, LANES).astype(BF)
    mixed = jnp.dot(high, results, preferred_element_type=F32) * 256.0
    mixed = mixed + jnp.dot(low, results, preferred_element_type=F32)
    mixed = (mixed / total).astype(BF)
    for i in range(DP):
        outp[i] = mixed[i * 16 : (i + 1) * 16]
    copies = []
    for d in range(1, DP):
        to = lax.rem(q + d, DP)
        copies.append(remote(outp.at[to], fin.at[q], fs.at[d - 1], fr.at[d - 1], {"dp": to}))
        copies[-1].start()
    out_ref[q] = outp[q]
    for d in range(1, DP):
        copies[d - 1].wait()
        src = lax.rem(q + DP - d, DP)
        out_ref[src] = fin[src]


def per_device(tokens, dest_ids, gate_fixed, gate_up, down):
    own = tokens[0].reshape(4, DP, 4, LANES).transpose(1, 0, 2, 3).reshape(DP, 16, LANES)
    gates = gate_fixed[0]
    routes = jnp.concatenate([dest_ids[0], gates >> 8, gates & 255], axis=1)
    routes = jnp.pad(routes, ((0, 0), (0, LANES - 3 * TOP))).astype(BF)
    routes = jnp.broadcast_to(routes[None, :, None, :], (DP, 4, 4, LANES)).reshape(DP, 16, LANES)
    msg = jnp.concatenate([own, routes], axis=1)
    dma = pltpu.SemaphoreType.DMA
    out = pl.pallas_call(
        kernel,
        out_shape=jax.ShapeDtypeStruct((DP, 16, LANES), BF),
        in_specs=[
            pl.BlockSpec(memory_space=pltpu.VMEM),
            pl.BlockSpec(memory_space=pl.ANY),
            pl.BlockSpec(memory_space=pl.ANY),
        ],
        out_specs=pl.BlockSpec(memory_space=pltpu.VMEM),
        scratch_shapes=[
            pltpu.VMEM((DP, 32, LANES), BF),
            pltpu.VMEM(gate_up.shape[1:], BF),
            pltpu.VMEM(down.shape[1:], BF),
            pltpu.VMEM((PEERS, 8, LANES), BF),
            pltpu.VMEM((DP, PEERS, 8, LANES), BF),
            pltpu.VMEM((PEERS * 2, QUARTER), BF),
            pltpu.VMEM((DP, PEERS * 2, QUARTER), BF),
            pltpu.VMEM((DP, PEERS * 2, QUARTER), BF),
            pltpu.VMEM((PEERS, 8, LANES), BF),
            pltpu.VMEM((PEERS, 8, LANES), BF),
            pltpu.VMEM((DP, 16, LANES), BF),
            pltpu.VMEM((DP, 16, LANES), BF),
            dma((2,)), dma((3,)), dma((3,)), dma, dma, dma((3,)), dma((3,)),
            dma((3,)), dma((3,)), dma, dma, dma((3,)), dma((3,)), dma((2,)),
        ],
        compiler_params=pltpu.CompilerParams(collective_id=0, has_side_effects=True),
        name="routed_experts",
    )(msg, gate_up[0], down[0])
    return out.reshape(DP, 4, 4, LANES).transpose(1, 0, 2, 3).reshape(1, 4, DP * QUARTER)


def solution(mesh):
    return jax.shard_map(
        per_device,
        mesh=mesh,
        in_specs=(
            P("ep", "dp", None),
            P("ep", "dp", None),
            P("ep", "dp", None),
            P("ep", None, "dp", None),
            P("ep", "dp", None),
        ),
        out_specs=P("ep", "dp", None),
        check_vma=False,
    )
```

time: 183 us -> 78.9 us (0.43)
  Pallas kernels: 0 us -> 75 us
  blocking collectives: 72.3 us -> 0 us
  waiting for transfers between devices: 71 us -> 0 us
  between operations: 14.2 us -> 0.02 us
  local copies, waits for them, and re-layouts: 11 us -> 2.1 us
  starting transfers between devices: 6.45 us -> 0 us
  matrix products: 4.21 us -> 0 us
    pallas_call x0 -> x1, Pallas kernels: none -> 75 us  [per_device(): pl.pallas_call(kernel, out_shape=jax.ShapeDtypeStruct((DP, 16, LANES), BF...]
    all_to_all x1 -> x0, blocking collectives: 53.9 us -> none  [per_device(): lax.all_to_all(send_block, 'ep', split_axis=0, concat_axis=0, tiled=True)]
    unnamed x2 -> x0, waiting for transfers between devices: 40.3 us -> none
    all_to_all x1 -> x0, waiting for transfers between devices: 30.6 us -> none  [per_device(): lax.all_to_all(own_out.reshape(rows.shape[0], rows.shape[1], -1), 'ep', s...]
    all_gather x2 -> x0, blocking collectives: 18.4 us -> none  [the longest x1 9.3 us: per_device(): column_table = lax.all_gather(route_table, 'dp', axis=0, tiled=True)]
    all_to_all x1 -> x0, starting transfers between devices: 6.41 us -> none  [per_device(): lax.all_to_all(own_out.reshape(rows.shape[0], rows.shape[1], -1), 'ep', s...]
    dot_general x2 -> x0, matrix products: 4.21 us -> none  [the longest x1 2.57 us: feed_forward(): jnp.dot(hidden, lower, preferred_element_type=jnp.float32)]
    scatter x1 -> x0, local copies, waits for them, and re-layouts: 3.36 us -> none  [per_device(): send_block = jnp.zeros((peer_count * capacity, width), jnp.bfloat16).at[s...]
  transfers between devices with their start and end apart: 2 -> 0, of which waited for: 2 -> 0; matrix products, arithmetic and copies ran while one was open for 1% -> 0% of each run, Pallas kernels for 0% -> 0%
where the time goes in v2:
time: 78.9 us; the launch traced here: 78.6 us
  Pallas kernels  75 us (95%)
  local copies, waits for them, and re-layouts  2.1 us (3%)
  other arithmetic  1.4 us (2%)
    pallas_call x1, Pallas kernels, per_device(): pl.pallas_call(kernel, out_shape=jax.ShapeDtypeStruct((DP, 16, LANES), BF...  75 us

profile of v2, /device:TPU:1, one launch (start us, length us, event | category | flops | bytes accessed | tf_op | source)
XLA Modules:
  0.0 78.6 jit_solution(7293034044741207646)
XLA Ops:
  0.0 0.7 fusion.3
  0.7 0.1 fusion.6
  0.8 0.7 reshape_squeeze.3
  1.5 0.6 pad_maximum_fusion.msg_ref
  2.2 75.0 %routed_experts.1 = bf16[4,16,128]{2,1,0:T(8,128)(2,1)} custom-call(bf16[4,32,128]{2,1,0:T(8,128)(2,1)} %pad_maximum_fusion.msg_ref, bf16[2,192,2048]{2,1,0:T(8,128)(2,1)} %bitcast.15, bf16[192,2048]{1,0:T(8,128)(2,1)} %bitcast.16), custom_call_target="tpu_custom_call" | custom-call | tf_op jit(solution)/shard_map/routed_experts/pallas_call | solution.py:205
  77.2 0.7 copy.7
  77.9 0.6 reshape.20
  (3 shorter events, 0.0 us)

commit v3 on v2

v3 whole, which is shorter than its diff:
```python
import jax
import jax.numpy as jnp
from jax import lax
from jax.experimental import pallas as pl
from jax.experimental.pallas import tpu as pltpu
from jax.sharding import PartitionSpec as P

BF = jnp.bfloat16
F32 = jnp.float32
MESH = pl.DeviceIdType.MESH
PEERS = 128
DP = 4
TOP = 8
LANES = 128
QUARTER = 512
STRIDE = 43
GROUPS = 2
GROUP = PEERS // GROUPS


def iota(shape, dim):
    return lax.broadcasted_iota(jnp.int32, shape, dim)


def permutation(inverse):
    moved = iota((128, 128), 1 if inverse else 0)
    place = iota((128, 128), 0 if inverse else 1)
    home = (moved & 31) // 2 * 8 + (moved & 1) * 4 + moved // 32
    return jnp.where(home == place, 1.0, 0.0).astype(BF)


def remote(src, dst, send_sem, recv_sem, device):
    return pltpu.make_async_remote_copy(
        src_ref=src, dst_ref=dst, send_sem=send_sem, recv_sem=recv_sem,
        device_id=device, device_id_type=MESH,
    )


def kernel(
    tokens_ref, ids_ref, gates_ref, pair_hbm, lower_hbm, out_ref,
    msg, table_ref, got, pair, lower, send1, recv1, rows, part, pin, send2, back, outp, fin,
    local_sem, xs, xr, a_send, a_recv, gs, gr, rs, rr, b_send, b_recv, fs, fr, own_sem,
):
    q = lax.axis_index("dp")
    me = lax.axis_index("ep")
    load_pair = pltpu.make_async_copy(pair_hbm, pair, local_sem.at[0])
    load_lower = pltpu.make_async_copy(lower_hbm, lower, local_sem.at[1])
    load_pair.start()
    load_lower.start()

    barrier = pltpu.get_barrier_semaphore()
    for d in range(1, DP):
        pl.semaphore_signal(
            barrier, inc=1, device_id={"dp": lax.rem(q + d, DP)}, device_id_type=MESH
        )

    def greet(d, carry):
        pl.semaphore_signal(
            barrier, inc=1, device_id={"ep": lax.rem(me + d, PEERS)}, device_id_type=MESH
        )
        return carry

    lax.fori_loop(1, PEERS, greet, 0)

    table_ref[...] = jnp.zeros(table_ref.shape, F32)
    table_ref[:, 0:TOP] = ids_ref[...].astype(F32)
    table_ref[:, TOP : 2 * TOP] = (gates_ref[...] >> 8).astype(F32)
    table_ref[:, 2 * TOP : 3 * TOP] = (gates_ref[...] & 255).astype(F32)
    routes = jnp.concatenate([table_ref[...]] * 4, axis=0).astype(BF)
    for i in range(DP):
        pieces = [
            tokens_ref[:, i * QUARTER + j * LANES : i * QUARTER + (j + 1) * LANES].astype(F32)
            for j in range(4)
        ]
        msg[i, 0:16] = jnp.concatenate(pieces, axis=0).astype(BF)
        msg[i, 16:32] = routes
    pl.semaphore_wait(barrier, DP - 1 + PEERS - 1)
    copies = []
    for d in range(1, DP):
        to = lax.rem(q + d, DP)
        copies.append(
            remote(msg.at[to], got.at[q], xs.at[d - 1], xr.at[d - 1], {"dp": to})
        )
        copies[-1].start()
    got[q] = msg[q]
    for copy in copies:
        copy.wait()

    tok = jnp.concatenate([got[i, 0:16, :] for i in range(DP)], axis=0)
    table = jnp.concatenate([got[i, 16:32, :].astype(F32) for i in range(DP)], axis=0)
    wide = (64, PEERS * 8)
    column = iota(wide, 1)
    expert = (column // 8).astype(F32)
    named = jnp.zeros(wide, F32)
    high = jnp.zeros(wide, F32)
    low = jnp.zeros(wide, F32)
    total = jnp.zeros((64, 1), F32)
    for k in range(TOP):
        same = table[:, k : k + 1] == expert
        hi, lo = table[:, TOP + k : TOP + k + 1], table[:, 2 * TOP + k : 2 * TOP + k + 1]
        total = total + (hi * 256.0 + lo)
        named = jnp.where(same, 1.0, named)
        high = jnp.where(same, hi, high)
        low = jnp.where(same, lo, low)
    line, other = iota((64, 64), 0), iota((64, 64), 1)
    before = other // 16 * 4 + (other & 3) < line // 16 * 4 + (line & 3)
    earlier = jnp.where(before & ((other // 4 & 3) == 0), 1.0, 0.0).astype(BF)
    rank = jnp.dot(earlier, named.astype(BF), preferred_element_type=F32)
    slot = ((column // 4) & 1).astype(F32)
    live = (rank == slot) & ((iota(wide, 0) // 4 & 3) == (column & 3))
    pick = jnp.where(live, named, 0.0)
    high = jnp.where(live, high, 0.0).astype(BF)
    low = jnp.where(live, low, 0.0).astype(BF)
    packed = jnp.dot(pick.T.astype(BF), tok, preferred_element_type=F32)
    send1[...] = packed.reshape(PEERS, 8, LANES).astype(BF)

    for g in range(GROUPS):

        def dispatch(i, carry):
            to = lax.rem(me + i * STRIDE, PEERS)
            remote(send1.at[to], recv1.at[q, i], a_send.at[g], a_recv.at[g], {"ep": to}).start()
            return carry

        lax.fori_loop(max(1, g * GROUP), (g + 1) * GROUP, dispatch, 0)
    own = pltpu.make_async_copy(send1.at[me], recv1.at[q, 0], own_sem.at[0])
    own.start()
    own.wait()

    gathers = {}
    for g in range(GROUPS):
        first = max(1, g * GROUP)
        span = pl.ds(first, (g + 1) * GROUP - first)
        remote(
            send1.at[span], recv1.at[q, span], a_send.at[g], a_recv.at[g],
            {"ep": lax.rem(me + 1, PEERS)},
        ).wait()
        span = pl.ds(g * GROUP, GROUP)
        for d in (2, 1, 3):
            to = lax.rem(q + d, DP)
            gathers[g, d] = remote(
                recv1.at[q, span], recv1.at[q, span], gs.at[d - 1, g], gr.at[d - 1, g], {"dp": to}
            )
            gathers[g, d].start()
    load_pair.wait()
    load_lower.wait()
    order = permutation(False)
    back_order = permutation(True)
    contract = (((1,), (1,)), ((), ()))
    reduces = {}

    def experts(g):
        gate = jnp.zeros((GROUP * 2, pair.shape[1]), F32)
        upper = jnp.zeros((GROUP * 2, pair.shape[1]), F32)
        for d in (0, 1, 3, 2):
            if d:
                gathers[g, d].wait()
            src = lax.rem(q + DP - d, DP)
            for b in range(GROUP // 16):
                start = g * GROUP + b * 16
                block = recv1[src, start : start + 16].astype(F32).reshape(128, LANES).astype(BF)
                moved = jnp.dot(order, block, preferred_element_type=F32).astype(BF)
                for j in range(4):
                    rows[g, b * 32 : (b + 1) * 32, j * LANES : (j + 1) * LANES] = moved[
                        j * 32 : (j + 1) * 32
                    ]
            x = rows[g]
            features = pl.ds(pl.multiple_of(src * QUARTER, QUARTER), QUARTER)
            gate = gate + lax.dot_general(
                x, pair[0, :, features], contract, preferred_element_type=F32
            )
            upper = upper + lax.dot_general(
                x, pair[1, :, features], contract, preferred_element_type=F32
            )
        hidden = (gate / (1.0 + jnp.exp(-gate)) * upper).astype(BF)
        for d in (2, 1, 3, 0):
            to = lax.rem(q + d, DP)
            features = pl.ds(pl.multiple_of(to * QUARTER, QUARTER), QUARTER)
            part[g, to] = jnp.dot(hidden, lower[:, features], preferred_element_type=F32).astype(BF)
            if d:
                reduces[g, d] = remote(
                    part.at[g, to], pin.at[g, q], rs.at[d - 1, g], rr.at[d - 1, g], {"dp": to}
                )
                reduces[g, d].start()

    def finish(g):
        for d in (1, 3, 2):
            reduces[g, d].wait()
        for b in range(GROUP // 16):
            lines = slice(b * 32, (b + 1) * 32)
            added = part[g, q, lines].astype(F32)
            for d in range(1, DP):
                added = added + pin[g, lax.rem(q + DP - d, DP), lines].astype(F32)
            added = added.astype(BF)
            stacked = jnp.concatenate(
                [added[:, j * LANES : (j + 1) * LANES] for j in range(4)], axis=0
            )
            moved = jnp.dot(back_order, stacked, preferred_element_type=F32)
            start = g * GROUP + b * 16
            send2[start : start + 16] = moved.reshape(16, 8, LANES).astype(BF)

        def giveback(i, carry):
            to = lax.rem(me + i * (PEERS - STRIDE), PEERS)
            remote(send2.at[i], back.at[me], b_send, b_recv, {"ep": to}).start()
            return carry

        lax.fori_loop(max(1, g * GROUP), (g + 1) * GROUP, giveback, 0)

    for g in range(GROUPS):
        experts(g)
        if g:
            finish(g - 1)
    finish(GROUPS - 1)
    own = pltpu.make_async_copy(send2.at[0], back.at[me], own_sem.at[1])
    own.start()
    own.wait()
    whole = pl.ds(0, PEERS - 1)
    remote(
        send2.at[whole], back.at[whole], b_send, b_recv, {"ep": lax.rem(me + 1, PEERS)}
    ).wait()

    results = back[...].astype(F32).reshape(PEERS * 8, LANES).astype(BF)
    mixed = jnp.dot(high, results, preferred_element_type=F32) * 256.0
    mixed = mixed + jnp.dot(low, results, preferred_element_type=F32)
    mixed = (mixed / total).astype(BF)
    for i in range(DP):
        outp[i] = mixed[i * 16 : (i + 1) * 16]
    copies = []
    for d in range(1, DP):
        to = lax.rem(q + d, DP)
        copies.append(remote(outp.at[to], fin.at[q], fs.at[d - 1], fr.at[d - 1], {"dp": to}))
        copies[-1].start()
    for d in range(DP):
        if d:
            copies[d - 1].wait()
        src = lax.rem(q + DP - d, DP)
        value = (fin[src] if d else outp[q]).astype(F32)
        for j in range(4):
            features = pl.ds(pl.multiple_of(src * QUARTER + j * LANES, LANES), LANES)
            out_ref[:, features] = value[j * 4 : (j + 1) * 4].astype(BF)


def per_device(tokens, dest_ids, gate_fixed, gate_up, down):
    dma = pltpu.SemaphoreType.DMA
    out = pl.pallas_call(
        kernel,
        out_shape=jax.ShapeDtypeStruct((4, DP * QUARTER), BF),
        in_specs=[
            pl.BlockSpec(memory_space=pltpu.VMEM),
            pl.BlockSpec(memory_space=pltpu.VMEM),
            pl.BlockSpec(memory_space=pltpu.VMEM),
            pl.BlockSpec(memory_space=pl.ANY),
            pl.BlockSpec(memory_space=pl.ANY),
        ],
        out_specs=pl.BlockSpec(memory_space=pltpu.VMEM),
        scratch_shapes=[
            pltpu.VMEM((DP, 32, LANES), BF),
            pltpu.VMEM((4, LANES), F32),
            pltpu.VMEM((DP, 32, LANES), BF),
            pltpu.VMEM(gate_up.shape[1:], BF),
            pltpu.VMEM(down.shape[1:], BF),
            pltpu.VMEM((PEERS, 8, LANES), BF),
            pltpu.VMEM((DP, PEERS, 8, LANES), BF),
            pltpu.VMEM((GROUPS, GROUP * 2, QUARTER), BF),
            pltpu.VMEM((GROUPS, DP, GROUP * 2, QUARTER), BF),
            pltpu.VMEM((GROUPS, DP, GROUP * 2, QUARTER), BF),
            pltpu.VMEM((PEERS, 8, LANES), BF),
            pltpu.VMEM((PEERS, 8, LANES), BF),
            pltpu.VMEM((DP, 16, LANES), BF),
            pltpu.VMEM((DP, 16, LANES), BF),
            dma((2,)), dma((3,)), dma((3,)), dma((GROUPS,)), dma((GROUPS,)),
            dma((3, GROUPS)), dma((3, GROUPS)), dma((3, GROUPS)), dma((3, GROUPS)),
            dma, dma, dma((3,)), dma((3,)), dma((2,)),
        ],
        compiler_params=pltpu.CompilerParams(collective_id=0, has_side_effects=True),
        name="routed_experts",
    )(tokens[0], dest_ids[0], gate_fixed[0], gate_up[0], down[0])
    return out[None]


def solution(mesh):
    return jax.shard_map(
        per_device,
        mesh=mesh,
        in_specs=(
            P("ep", "dp", None),
            P("ep", "dp", None),
            P("ep", "dp", None),
            P("ep", None, "dp", None),
            P("ep", "dp", None),
        ),
        out_specs=P("ep", "dp", None),
        check_vma=False,
    )
```

time: 78.9 us -> 70.2 us (0.89)
  Pallas kernels: 75 us -> 68.6 us
  other arithmetic: 1.4 us -> 0 us
    pallas_call x1, Pallas kernels: 75 us -> 68.6 us  [per_device(): pl.pallas_call(kernel, out_shape=jax.ShapeDtypeStruct((4, DP * QUARTER),...]
    unnamed x0 -> x1, local copies, waits for them, and re-layouts: none -> 1.33 us
where the time goes in v3:
time: 70.2 us; the launch traced here: 70 us
  Pallas kernels  68.6 us (98%)
  local copies, waits for them, and re-layouts  1.33 us (2%)
    pallas_call x1, Pallas kernels, per_device(): pl.pallas_call(kernel, out_shape=jax.ShapeDtypeStruct((4, DP * QUARTER),...  68.6 us

profile of v3, /device:TPU:1, one launch (start us, length us, event | category | flops | bytes accessed | tf_op | source)
XLA Modules:
  0.0 70.0 jit_solution(8429387751425790033)
XLA Ops:
  0.0 68.6 %routed_experts.1 = bf16[4,2048]{1,0:T(4,128)(2,1)} custom-call(bf16[4,2048]{1,0:T(4,128)(2,1)} %bitcast.9, s32[4,8]{1,0:T(4,128)} %bitcast.10, s32[4,8]{1,0:T(4,128)} %bitcast.11, bf16[2,192,2048]{2,1,0:T(8,128)(2,1)} %bitcast.6, bf16[192,2048]{1,0:T(8,128)(2,1)} %bitcast.7), custom_call_target="tpu_custom_call" | custom-call | tf_op jit(solution)/shard_map/routed_experts/pallas_call | solution.py:244
  68.6 1.3 %copy.7 = bf16[1,4,2048]{2,1,0:T(4,128)(2,1)} copy(bf16[1,4,2048]{2,1,0:T(4,128)(2,1)} %bitcast.8) | data formatting | bytes 32768

commit v4 on v3

--- a/solution.py
+++ b/solution.py
@@ -14,7 +14,7 @@
 LANES = 128
 QUARTER = 512
 STRIDE = 43
-GROUPS = 2
+GROUPS = 4
 GROUP = PEERS // GROUPS
 
 
@@ -39,7 +39,7 @@
 def kernel(
     tokens_ref, ids_ref, gates_ref, pair_hbm, lower_hbm, out_ref,
     msg, table_ref, got, pair, lower, send1, recv1, rows, part, pin, send2, back, outp, fin,
-    local_sem, xs, xr, a_send, a_recv, gs, gr, rs, rr, b_send, b_recv, fs, fr, own_sem,
+    local_sem, xs, xr, a_send, a_recv, gs, gr, rs, rr, b_send, b_recv, fs, fr, own_sem, line_sem, twin_sem,
 ):
     q = lax.axis_index("dp")
     me = lax.axis_index("ep")
@@ -54,13 +54,12 @@
             barrier, inc=1, device_id={"dp": lax.rem(q + d, DP)}, device_id_type=MESH
         )
 
-    def greet(d, carry):
-        pl.semaphore_signal(
-            barrier, inc=1, device_id={"ep": lax.rem(me + d, PEERS)}, device_id_type=MESH
-        )
-        return carry
-
-    lax.fori_loop(1, PEERS, greet, 0)
+    z, y, core = me // 16, me // 2 % 8, me % 2
+    line = [lax.rem(me + 16 * d, PEERS) for d in range(1, 8)]
+    across = [z * 16 + lax.rem(y + d, 8) * 2 + core for d in range(1, 8)]
+    twin = z * 16 + y * 2 + (1 - core)
+    for to in line + across + [twin]:
+        pl.semaphore_signal(barrier, inc=1, device_id={"ep": to}, device_id_type=MESH)
 
     table_ref[...] = jnp.zeros(table_ref.shape, F32)
     table_ref[:, 0:TOP] = ids_ref[...].astype(F32)
@@ -74,7 +73,9 @@
         ]
         msg[i, 0:16] = jnp.concatenate(pieces, axis=0).astype(BF)
         msg[i, 16:32] = routes
-    pl.semaphore_wait(barrier, DP - 1 + PEERS - 1)
+    pl.semaphore_wait(barrier, DP - 1 + 15)
+    for to in line:
+        pl.semaphore_signal(line_sem, inc=1, device_id={"ep": to}, device_id_type=MESH)
     copies = []
     for d in range(1, DP):
         to = lax.rem(q + d, DP)
@@ -83,6 +84,8 @@
         )
         copies[-1].start()
     got[q] = msg[q]
+    pl.semaphore_wait(line_sem, 7)
+    pl.semaphore_signal(twin_sem, inc=1, device_id={"ep": twin}, device_id_type=MESH)
     for copy in copies:
         copy.wait()
 
@@ -102,8 +105,8 @@
         named = jnp.where(same, 1.0, named)
         high = jnp.where(same, hi, high)
         low = jnp.where(same, lo, low)
-    line, other = iota((64, 64), 0), iota((64, 64), 1)
-    before = other // 16 * 4 + (other & 3) < line // 16 * 4 + (line & 3)
+    this, other = iota((64, 64), 0), iota((64, 64), 1)
+    before = other // 16 * 4 + (other & 3) < this // 16 * 4 + (this & 3)
     earlier = jnp.where(before & ((other // 4 & 3) == 0), 1.0, 0.0).astype(BF)
     rank = jnp.dot(earlier, named.astype(BF), preferred_element_type=F32)
     slot = ((column // 4) & 1).astype(F32)
@@ -113,6 +116,8 @@
     low = jnp.where(live, low, 0.0).astype(BF)
     packed = jnp.dot(pick.T.astype(BF), tok, preferred_element_type=F32)
     send1[...] = packed.reshape(PEERS, 8, LANES).astype(BF)
+
+    pl.semaphore_wait(twin_sem, 1)
 
     for g in range(GROUPS):
 
@@ -270,6 +275,7 @@
             dma((2,)), dma((3,)), dma((3,)), dma((GROUPS,)), dma((GROUPS,)),
             dma((3, GROUPS)), dma((3, GROUPS)), dma((3, GROUPS)), dma((3, GROUPS)),
             dma, dma, dma((3,)), dma((3,)), dma((2,)),
+            pltpu.SemaphoreType.REGULAR, pltpu.SemaphoreType.REGULAR,
         ],
         compiler_params=pltpu.CompilerParams(collective_id=0, has_side_effects=True),
         name="routed_experts",

time: 70.2 us -> 65.9 us (0.939)
  Pallas kernels: 68.6 us -> 64.3 us
    pallas_call x1, Pallas kernels: 68.6 us -> 64.3 us  [per_device(): pl.pallas_call(kernel, out_shape=jax.ShapeDtypeStruct((4, DP * QUARTER),...]
where the time goes in v4:
time: 65.9 us; the launch traced here: 65.7 us
  Pallas kernels  64.3 us (98%)
  local copies, waits for them, and re-layouts  1.33 us (2%)
    pallas_call x1, Pallas kernels, per_device(): pl.pallas_call(kernel, out_shape=jax.ShapeDtypeStruct((4, DP * QUARTER),...  64.3 us
    unnamed x1, local copies, waits for them, and re-layouts  1.33 us

profile of v4, /device:TPU:1, one launch (start us, length us, event | category | flops | bytes accessed | tf_op | source)
XLA Modules:
  0.0 65.7 jit_solution(16495996867288620153)
XLA Ops:
  0.0 64.3 %routed_experts.1 = bf16[4,2048]{1,0:T(4,128)(2,1)} custom-call(bf16[4,2048]{1,0:T(4,128)(2,1)} %bitcast.9, s32[4,8]{1,0:T(4,128)} %bitcast.10, s32[4,8]{1,0:T(4,128)} %bitcast.11, bf16[2,192,2048]{2,1,0:T(8,128)(2,1)} %bitcast.6, bf16[192,2048]{1,0:T(8,128)(2,1)} %bitcast.7), custom_call_target="tpu_custom_call" | custom-call | tf_op jit(solution)/shard_map/routed_experts/pallas_call | solution.py:249
  64.4 1.3 %copy.7 = bf16[1,4,2048]{2,1,0:T(4,128)(2,1)} copy(bf16[1,4,2048]{2,1,0:T(4,128)(2,1)} %bitcast.8) | data formatting | bytes 32768

commit v5 on v4

--- a/solution.py
+++ b/solution.py
@@ -14,7 +14,7 @@
 LANES = 128
 QUARTER = 512
 STRIDE = 43
-GROUPS = 4
+GROUPS = 2
 GROUP = PEERS // GROUPS
 
 
@@ -39,7 +39,8 @@
 def kernel(
     tokens_ref, ids_ref, gates_ref, pair_hbm, lower_hbm, out_ref,
     msg, table_ref, got, pair, lower, send1, recv1, rows, part, pin, send2, back, outp, fin,
-    local_sem, xs, xr, a_send, a_recv, gs, gr, rs, rr, b_send, b_recv, fs, fr, own_sem, line_sem, twin_sem,
+    local_sem, xs, xr, a_send, a_recv, gs, gr, rs, rr, b_send, b_recv, fs, fr, own_sem, line_sem, twin_sem, hs, hr,
+    hop, us, ur, ws, wr,
 ):
     q = lax.axis_index("dp")
     me = lax.axis_index("ep")
@@ -132,6 +133,20 @@
     own.wait()
 
     gathers = {}
+    relays = {}
+    half = GROUP // 2
+
+    def relay(g):
+        for d in (1, 3):
+            gathers[g, d].wait_recv()
+            src = lax.rem(q + DP - d, DP)
+            span = pl.ds(g * GROUP + (0 if d == 1 else half), half)
+            relays[g, d] = remote(
+                recv1.at[src, span], recv1.at[src, span], hs.at[d // 2, g], hr.at[d // 2, g],
+                {"dp": lax.rem(q + d, DP)},
+            )
+            relays[g, d].start()
+
     for g in range(GROUPS):
         first = max(1, g * GROUP)
         span = pl.ds(first, (g + 1) * GROUP - first)
@@ -140,33 +155,46 @@
             {"ep": lax.rem(me + 1, PEERS)},
         ).wait()
         span = pl.ds(g * GROUP, GROUP)
-        for d in (2, 1, 3):
+        for d in (1, 3):
             to = lax.rem(q + d, DP)
             gathers[g, d] = remote(
                 recv1.at[q, span], recv1.at[q, span], gs.at[d - 1, g], gr.at[d - 1, g], {"dp": to}
             )
             gathers[g, d].start()
+        if g:
+            relay(g - 1)
     load_pair.wait()
     load_lower.wait()
     order = permutation(False)
     back_order = permutation(True)
     contract = (((1,), (1,)), ((), ()))
-    reduces = {}
+    reduces, hops, sums = {}, {}, {}
+    first_half, second_half = pl.ds(0, GROUP), pl.ds(GROUP, GROUP)
 
     def experts(g):
         gate = jnp.zeros((GROUP * 2, pair.shape[1]), F32)
         upper = jnp.zeros((GROUP * 2, pair.shape[1]), F32)
         for d in (0, 1, 3, 2):
-            if d:
-                gathers[g, d].wait()
+            if g == 0 and d == 1:
+                relay(GROUPS - 1)
+            if d == 2:
+                for copy in (relays[g, 1], relays[g, 3]):
+                    copy.wait()
+            elif d:
+                gathers[g, d].wait_send()
             src = lax.rem(q + DP - d, DP)
+            blocks = []
             for b in range(GROUP // 16):
                 start = g * GROUP + b * 16
-                block = recv1[src, start : start + 16].astype(F32).reshape(128, LANES).astype(BF)
-                moved = jnp.dot(order, block, preferred_element_type=F32).astype(BF)
+                block = recv1[src, start : start + 16].astype(F32).reshape(128, LANES)
+                blocks.append(block.astype(BF))
+            moved = jnp.dot(
+                order, jnp.concatenate(blocks, axis=1), preferred_element_type=F32
+            ).astype(BF)
+            for b in range(GROUP // 16):
                 for j in range(4):
                     rows[g, b * 32 : (b + 1) * 32, j * LANES : (j + 1) * LANES] = moved[
-                        j * 32 : (j + 1) * 32
+                        j * 32 : (j + 1) * 32, b * LANES : (b + 1) * LANES
                     ]
             x = rows[g]
             features = pl.ds(pl.multiple_of(src * QUARTER, QUARTER), QUARTER)
@@ -176,32 +204,63 @@
             upper = upper + lax.dot_general(
                 x, pair[1, :, features], contract, preferred_element_type=F32
             )
+        if g:
+            relay_sum(g - 1)
         hidden = (gate / (1.0 + jnp.exp(-gate)) * upper).astype(BF)
         for d in (2, 1, 3, 0):
             to = lax.rem(q + d, DP)
             features = pl.ds(pl.multiple_of(to * QUARTER, QUARTER), QUARTER)
             part[g, to] = jnp.dot(hidden, lower[:, features], preferred_element_type=F32).astype(BF)
-            if d:
-                reduces[g, d] = remote(
-                    part.at[g, to], pin.at[g, q], rs.at[d - 1, g], rr.at[d - 1, g], {"dp": to}
-                )
-                reduces[g, d].start()
+            for side in (1, 3):
+                if d == 2:
+                    lines = first_half if side == 1 else second_half
+                    hops[g, side] = remote(
+                        part.at[g, to, lines], hop.at[g, side // 2],
+                        us.at[side // 2, g], ur.at[side // 2, g], {"dp": lax.rem(q + side, DP)},
+                    )
+                    hops[g, side].start()
+                elif d == side:
+                    lines = second_half if side == 1 else first_half
+                    reduces[g, d] = remote(
+                        part.at[g, to, lines], pin.at[g, q, lines],
+                        rs.at[d - 1, g], rr.at[d - 1, g], {"dp": to},
+                    )
+                    reduces[g, d].start()
+
+    def relay_sum(g):
+        for d in (1, 3):
+            hops[g, d].wait()
+            to = lax.rem(q + d, DP)
+            lines = first_half if d == 1 else second_half
+            both = part[g, to, lines].astype(F32) + hop[g, d // 2].astype(F32)
+            part[g, to, lines] = both.astype(BF)
+            sums[g, d] = remote(
+                part.at[g, to, lines], pin.at[g, q, lines],
+                ws.at[d // 2, g], wr.at[d // 2, g], {"dp": to},
+            )
+            sums[g, d].start()
 
     def finish(g):
-        for d in (1, 3, 2):
+        for d in (1, 3):
             reduces[g, d].wait()
+            sums[g, d].wait()
+        blocks = []
         for b in range(GROUP // 16):
             lines = slice(b * 32, (b + 1) * 32)
             added = part[g, q, lines].astype(F32)
-            for d in range(1, DP):
+            for d in (1, 3):
                 added = added + pin[g, lax.rem(q + DP - d, DP), lines].astype(F32)
             added = added.astype(BF)
-            stacked = jnp.concatenate(
-                [added[:, j * LANES : (j + 1) * LANES] for j in range(4)], axis=0
-            )
-            moved = jnp.dot(back_order, stacked, preferred_element_type=F32)
+            blocks.append(
+                jnp.concatenate([added[:, j * LANES : (j + 1) * LANES] for j in range(4)], axis=0)
+            )
+        moved = jnp.dot(
+            back_order, jnp.concatenate(blocks, axis=1), preferred_element_type=F32
+        )
+        for b in range(GROUP // 16):
             start = g * GROUP + b * 16
-            send2[start : start + 16] = moved.reshape(16, 8, LANES).astype(BF)
+            block = moved[:, b * LANES : (b + 1) * LANES]
+            send2[start : start + 16] = block.reshape(16, 8, LANES).astype(BF)
 
         def giveback(i, carry):
             to = lax.rem(me + i * (PEERS - STRIDE), PEERS)
@@ -214,6 +273,7 @@
         experts(g)
         if g:
             finish(g - 1)
+    relay_sum(GROUPS - 1)
     finish(GROUPS - 1)
     own = pltpu.make_async_copy(send2.at[0], back.at[me], own_sem.at[1])
     own.start()
@@ -276,6 +336,9 @@
             dma((3, GROUPS)), dma((3, GROUPS)), dma((3, GROUPS)), dma((3, GROUPS)),
             dma, dma, dma((3,)), dma((3,)), dma((2,)),
             pltpu.SemaphoreType.REGULAR, pltpu.SemaphoreType.REGULAR,
+            dma((2, GROUPS)), dma((2, GROUPS)),
+            pltpu.VMEM((GROUPS, 2, GROUP, QUARTER), BF),
+            dma((2, GROUPS)), dma((2, GROUPS)), dma((2, GROUPS)), dma((2, GROUPS)),
         ],
         compiler_params=pltpu.CompilerParams(collective_id=0, has_side_effects=True),
         name="routed_experts",

time: 65.9 us -> 64.8 us (0.983)
  Pallas kernels: 64.3 us -> 63.2 us
    pallas_call x1, Pallas kernels: 64.3 us -> 63.2 us  [per_device(): pl.pallas_call(kernel, out_shape=jax.ShapeDtypeStruct((4, DP * QUARTER),...]
where the time goes in v5:
time: 64.8 us; the launch traced here: 64.5 us
  Pallas kernels  63.2 us (98%)
  local copies, waits for them, and re-layouts  1.33 us (2%)
    pallas_call x1, Pallas kernels, per_device(): pl.pallas_call(kernel, out_shape=jax.ShapeDtypeStruct((4, DP * QUARTER),...  63.2 us
    unnamed x1, local copies, waits for them, and re-layouts  1.33 us

profile of v5, /device:TPU:1, one launch (start us, length us, event | category | flops | bytes accessed | tf_op | source)
XLA Modules:
  0.0 64.5 jit_solution(16389412736922598395)
XLA Ops:
  0.0 63.2 %routed_experts.1 = bf16[4,2048]{1,0:T(4,128)(2,1)} custom-call(bf16[4,2048]{1,0:T(4,128)(2,1)} %bitcast.9, s32[4,8]{1,0:T(4,128)} %bitcast.10, s32[4,8]{1,0:T(4,128)} %bitcast.11, bf16[2,192,2048]{2,1,0:T(8,128)(2,1)} %bitcast.6, bf16[192,2048]{1,0:T(8,128)(2,1)} %bitcast.7), custom_call_target="tpu_custom_call" | custom-call | tf_op jit(solution)/shard_map/routed_experts/pallas_call | solution.py:309
  63.2 1.3 %copy.7 = bf16[1,4,2048]{2,1,0:T(4,128)(2,1)} copy(bf16[1,4,2048]{2,1,0:T(4,128)(2,1)} %bitcast.8) | data formatting | bytes 32768

commit v6 on v5

--- a/solution.py
+++ b/solution.py
@@ -120,6 +120,8 @@
 
     pl.semaphore_wait(twin_sem, 1)
 
+    own = pltpu.make_async_copy(send1.at[me], recv1.at[q, 0], own_sem.at[0])
+    own.start()
     for g in range(GROUPS):
 
         def dispatch(i, carry):
@@ -128,8 +130,6 @@
             return carry
 
         lax.fori_loop(max(1, g * GROUP), (g + 1) * GROUP, dispatch, 0)
-    own = pltpu.make_async_copy(send1.at[me], recv1.at[q, 0], own_sem.at[0])
-    own.start()
     own.wait()
 
     gathers = {}
@@ -274,9 +274,9 @@
         if g:
             finish(g - 1)
     relay_sum(GROUPS - 1)
-    finish(GROUPS - 1)
     own = pltpu.make_async_copy(send2.at[0], back.at[me], own_sem.at[1])
     own.start()
+    finish(GROUPS - 1)
     own.wait()
     whole = pl.ds(0, PEERS - 1)
     remote(

time: 64.8 us -> 64.8 us (level)
  no operation moved by 1% of the time
where the time goes in v6:
time: 64.8 us; the launch traced here: 64.5 us
  Pallas kernels  63.2 us (98%)
  local copies, waits for them, and re-layouts  1.33 us (2%)
    pallas_call x1, Pallas kernels, per_device(): pl.pallas_call(kernel, out_shape=jax.ShapeDtypeStruct((4, DP * QUARTER),...  63.2 us
    unnamed x1, local copies, waits for them, and re-layouts  1.33 us

profile of v6, /device:TPU:1, one launch (start us, length us, event | category | flops | bytes accessed | tf_op | source)
XLA Modules:
  0.0 64.5 jit_solution(13401746099899867407)
XLA Ops:
  0.0 63.2 %routed_experts.1 = bf16[4,2048]{1,0:T(4,128)(2,1)} custom-call(bf16[4,2048]{1,0:T(4,128)(2,1)} %bitcast.9, s32[4,8]{1,0:T(4,128)} %bitcast.10, s32[4,8]{1,0:T(4,128)} %bitcast.11, bf16[2,192,2048]{2,1,0:T(8,128)(2,1)} %bitcast.6, bf16[192,2048]{1,0:T(8,128)(2,1)} %bitcast.7), custom_call_target="tpu_custom_call" | custom-call | tf_op jit(solution)/shard_map/routed_experts/pallas_call | solution.py:309
  63.2 1.3 %copy.7 = bf16[1,4,2048]{2,1,0:T(4,128)(2,1)} copy(bf16[1,4,2048]{2,1,0:T(4,128)(2,1)} %bitcast.8) | data formatting | bytes 32768
